TPU v7x, 32 devices: a whole 2x2x4 slice. The times are simulated.
32 devices in a mesh: row: 4 (over y, x), col: 8 (over z, core).
Axes of the slice: x: 2, y: 2, z: 4, core: 2. Of those that a mesh axis runs over, the one named last changes fastest.
Arguments:
- ainv: float32 [24576, 24576], P('row', 'col'), may hold values from -0.0390625 to 0.0390625
- lpanel: float32 [24576, 1024], P(('row', 'col')), may hold values from -0.6 to 0.6
- dinv: float32 [1024, 512], P(('row', 'col')), may hold values from -6 to 6
- lmask: int32 [384, 2], P(('row', 'col')), may hold values 0 or 1
- hrows: float32 [24576, 1024], P(('row', 'col')), may hold values from -6 to 6
- hmask: int32 [384, 2], P(('row', 'col')), may hold values 0 or 1
- pole_weight: float32 [1], replicated, may hold values from 0.5 to 2
Outputs:
- offdiag: float32 [24576, 1024], P(('row', 'col'))
- diaginv: float32 [1024, 512], P(('row', 'col'))
- energy: float32 [24576], P(('row', 'col'))
All inputs are finite; a program needn't handle non-finite values. No bound on the sum of `lmask` or of `hmask` on one device may be relied on, other than what follows from the above.
Results may differ from a plain program's by a relative error of at most 0.00024.
Values sent between devices are 32-bit elements; how exact they have to be, the bound alone decides.
A program may use at most 192 MiB of HBM per device.

v0:
```python
import jax
import jax.numpy as jnp
from jax import lax
from jax.sharding import PartitionSpec as P


def from_root(block, axis, holder):
    block = jnp.where(lax.axis_index(axis) == holder, block, jnp.zeros_like(block))
    return lax.psum(block, axis)


def expand_local(mask, block_rows, supernode):
    count = mask.shape[0]
    full = jnp.broadcast_to(
        mask.astype(jnp.float32)[:, None, :, None], (count, block_rows, 2, supernode)
    )
    return full.reshape(count * block_rows, 2 * supernode)


def diag_blocks(left, right, supernode):
    total_rows = left.shape[0]
    blocks = jnp.einsum(
        "rsa,rsb->sab",
        left.reshape(total_rows, 2, supernode),
        right.reshape(total_rows, 2, supernode),
        precision=lax.Precision.HIGHEST,
    )
    return blocks.reshape(2 * supernode, supernode)


def local(ainv, lpanel, dinv, lmask, hrows, hmask, pole_weight):
    rows_local = lpanel.shape[0]
    supernode = lpanel.shape[1] // 2
    block_rows = rows_local // lmask.shape[0]
    pattern = expand_local(lmask, block_rows, supernode)
    lmasked = lpanel * pattern
    rowpanel = lax.all_gather(lmasked, "col", axis=0, tiled=True)
    ratio = lax.axis_size("col") // lax.axis_size("row")
    colindex = lax.axis_index("col")
    col_rows = ainv.shape[1]
    slab_piece = lax.dynamic_slice_in_dim(rowpanel, colindex % ratio * col_rows, col_rows, 0)
    colpanel = from_root(slab_piece, "row", colindex // ratio)
    partial_value = jnp.dot(
        ainv, colpanel, precision=lax.Precision.HIGHEST, preferred_element_type=jnp.float32
    )
    owned = lax.psum_scatter(partial_value, "col", scatter_dimension=0, tiled=True)
    diag_term = diag_blocks(lmasked, owned, supernode)
    diag_sum = lax.psum_scatter(diag_term, ("row", "col"), scatter_dimension=0, tiled=True)
    offdiag = -owned * pattern
    diaginv = dinv + diag_sum
    hpattern = expand_local(hmask, block_rows, supernode)
    energy = pole_weight[0] * jnp.sum(hrows * hpattern * offdiag, axis=1)
    return (offdiag, diaginv, energy)


def solution(mesh):
    in_specs = (
        P("row", "col"),
        P(("row", "col"), None),
        P(("row", "col"), None),
        P(("row", "col"), None),
        P(("row", "col"), None),
        P(("row", "col"), None),
        P(),
    )
    out_specs = (P(("row", "col"), None), P(("row", "col"), None), P(("row", "col")))
    return jax.shard_map(local, mesh=mesh, in_specs=in_specs, out_specs=out_specs, check_vma=False)
```

profile of v0, /device:TPU:0, one launch (start us, length us, event | category | flops | bytes accessed | tf_op | source)
XLA Modules:
  0.0 1365.5 jit_solution(3551844918401968590)
XLA Ops:
  7.2 0.0 all-gather.2.cloned.1.call-start
  7.2 0.7 convert_element_type.6
  7.9 0.1 copy.14
  8.0 0.9 broadcast_in_dim.6
  8.9 0.8 copy.24
  9.6 1.1 copy-done.1
  10.8 2.6 mul.21
  13.4 0.0 all-gather.2.cloned.1.call-update
  13.4 0.0 all-reduce.2.cloned.1.call-start
  13.5 222.6 %all-gather.2.cloned.1.call-done = f32[6144,1024]{1,0:T(8,128)} async-done(((f32[768,1024]{1,0:T(8,128)}), f32[6144,1024]{1,0:T(8,128)}) %all-gather.2.cloned.1.call-update) | async-done | bytes 25165840 | tf_op jit(solution)/shard_map/all_gather | solution.py:37
  236.1 12.1 dynamic-slice_select_fusion
  248.2 0.0 all-reduce.2.cloned.1.call-update
  248.3 0.0 reduce-scatter.3.cloned.1.call-start
  248.3 237.6 %all-reduce.2.cloned.1.call-done = f32[3072,1024]{1,0:T(8,128)} async-done(((f32[3072,1024]{1,0:T(8,128)}), f32[3072,1024]{1,0:T(8,128)}) %all-reduce.2.cloned.1.call-update) | async-done | bytes 12582928 | tf_op jit(solution)/shard_map/psum | solution.py:9
  485.9 477.5 %convolution_bitcast_fusion = f32[6144,1024]{0,1:T(8,128)} fusion(f32[3072,1024]{1,0:T(8,128)} %all-reduce.2.cloned.1.call-done, f32[6144,3072]{1,0:T(8,128)} %param.7), kind=kOutput, calls=%fused_computation | convolution fusion | flops 231928233984 | bytes 113246208 | tf_op jit(solution)/shard_map/dot_general | solution.py:43
  963.4 0.0 reduce-scatter.3.cloned.1.call-update
  963.5 0.0 reduce-scatter.5.cloned.1.call-start
  963.5 3.6 copy.23
  967.1 243.6 %reduce-scatter.3.cloned.1.call-done = f32[768,1024]{0,1:T(8,128)} async-done(((f32[6144,1024]{0,1:T(8,128)}), f32[768,1024]{0,1:T(8,128)}) %reduce-scatter.3.cloned.1.call-update) | async-done | bytes 3145744 | tf_op jit(solution)/shard_map/reduce_scatter | solution.py:46
  1210.7 9.3 fusion
  1220.1 0.0 reduce-scatter.5.cloned.1.call-update
  1220.1 2.4 copy.15
  1222.5 0.1 copy.18
  1222.6 0.9 broadcast_in_dim.8
  1223.5 2.4 copy.25
  1225.9 3.5 copy.20
  1229.4 3.7 copy.19
  1233.8 6.2 multiply_reduce_fusion
  1240.0 3.6 copy.21
  1243.5 0.6 broadcast_multiply_fusion
  1244.1 113.3 %reduce-scatter.5.cloned.1.call-done = f32[32,512]{1,0:T(8,128)} async-done(((f32[1024,512]{1,0:T(8,128)}), f32[32,512]{1,0:T(8,128)}) %reduce-scatter.5.cloned.1.call-update) | async-done | bytes 65552 | tf_op jit(solution)/shard_map/reduce_scatter | solution.py:48
  1357.5 1.5 add.19
  (8 shorter events, 0.0 us)
Async XLA Ops:
  7.2 229.0 %all-gather.2.cloned.1.call-start = ((), (), s32[]{:S(2)}) async-start(), calls=%async_computation.2 | async-start | bytes 28311552 | tf_op jit(solution)/shard_map/all_gather | solution.py:37
  8.9 1.9 copy-start.1
  13.4 472.5 %all-reduce.2.cloned.1.call-start = ((), (), s32[]{:S(2)}) async-start(), calls=%async_computation.3 | async-start | bytes 25165824 | tf_op jit(solution)/shard_map/psum | solution.py:9
  248.3 962.4 %reduce-scatter.3.cloned.1.call-start = ((), (), s32[]{:S(2)}) async-start(), calls=%async_computation.4 | async-start | bytes 28311552 | tf_op jit(solution)/shard_map/reduce_scatter | solution.py:46
  963.5 394.0 %reduce-scatter.5.cloned.1.call-start = ((), (), s32[]{:S(2)}) async-start(), calls=%async_computation.5 | async-start | bytes 2162688 | tf_op jit(solution)/shard_map/reduce_scatter | solution.py:48
  1220.1 2.4 copy-start.3
  1229.4 4.3 copy-start
  1240.0 117.5 %copy-start.2 = (f32[32,512]{1,0:T(8,128)S(1)}, f32[32,512]{1,0:T(8,128)}, u32[]{:S(2)}) copy-start(f32[32,512]{1,0:T(8,128)} %param.9) | copy-start | bytes 196612
Sparse Core Ops, SparseCore 0:
  13.5 222.5 all-gather.1
  248.4 237.4 all-reduce.1
  963.6 247.0 reduce-scatter.2
  1220.2 137.2 reduce-scatter.4
where the time goes:
time: 1370 us
  waiting for transfers between devices  817 us (60%)
  matrix products  487 us (36%)
  other arithmetic  23.6 us (2%)
  local copies, waits for them, and re-layouts  23.1 us (2%)
  between operations  14.5 us (1%)
    dot_general x1, matrix products, local(): jnp.dot(ainv, colpanel, precision=lax.Precision.HIGHEST, preferred_elemen...  478 us
    reduce_scatter x1, waiting for transfers between devices, local(): lax.psum_scatter(partial_value, 'col', scatter_dimension=0, tiled=True)  244 us
    psum x1, waiting for transfers between devices, from_root(): return lax.psum(block, axis)  238 us
    all_gather x1, waiting for transfers between devices, local(): rowpanel = lax.all_gather(lmasked, 'col', axis=0, tiled=True)  223 us
    reduce_scatter x1, waiting for transfers between devices, local(): lax.psum_scatter(diag_term, ('row', 'col'), scatter_dimension=0, tiled=True)  113 us
  transfers between devices with their start and end apart: 4, of which 4 were waited for; matrix products, arithmetic and copies ran while one was open for 2% of the time, Pallas kernels for 0%

commit v1 on v0

v1 whole, which is shorter than its diff:
```python
import jax
import jax.numpy as jnp
from jax import lax
from jax.sharding import PartitionSpec as P


def expand_local(mask, block_rows, columns):
    count = mask.shape[0]
    full = jnp.broadcast_to(
        mask.astype(jnp.float32)[:, None, None], (count, block_rows, columns)
    )
    return full.reshape(count * block_rows, columns)


def to_grid_column(block):
    rows, cols = lax.axis_size("row"), lax.axis_size("col")
    pairs = [(g, (g % rows) * cols + g // rows) for g in range(rows * cols)]
    return lax.ppermute(block, ("row", "col"), pairs)


def local(ainv, lpanel, dinv, lmask, hrows, hmask, pole_weight):
    rows_local = lpanel.shape[0]
    supernode = lpanel.shape[1] // 2
    block_rows = rows_local // lmask.shape[0]
    rows, cols = lax.axis_size("row"), lax.axis_size("col")
    owned_diag = dinv.shape[0]
    offdiags, diags, energy = [], [], 0.0
    for s in range(2):
        at = slice(s * supernode, (s + 1) * supernode)
        pattern = expand_local(lmask[:, s], block_rows, supernode)
        lmasked = lpanel[:, at] * pattern
        colpanel = lax.all_gather(to_grid_column(lmasked), "row", axis=0, tiled=True)
        partial_value = jnp.dot(
            ainv, colpanel, precision=lax.Precision.HIGH, preferred_element_type=jnp.float32
        )
        owned = lax.psum_scatter(partial_value, "col", scatter_dimension=0, tiled=True)
        term = lax.dot_general(
            lmasked, owned, (((0,), (0,)), ((), ())), precision=lax.Precision.HIGH,
            preferred_element_type=jnp.float32,
        )
        half = supernode // (cols * owned_diag)
        term = term.reshape(half, cols, owned_diag, supernode).transpose(1, 0, 2, 3)
        diags.append(lax.psum_scatter(term, "col", scatter_dimension=0, tiled=False))
        offdiag = -owned * pattern
        offdiags.append(offdiag)
        hpattern = expand_local(hmask[:, s], block_rows, supernode)
        energy = energy + jnp.sum(hrows[:, at] * hpattern * offdiag, axis=1)
    diag = jnp.concatenate(diags, axis=0)
    diag_sum = lax.psum_scatter(diag, "row", scatter_dimension=0, tiled=False)
    return (jnp.concatenate(offdiags, axis=1), dinv + diag_sum, pole_weight[0] * energy)


def solution(mesh):
    in_specs = (
        P("row", "col"),
        P(("row", "col"), None),
        P(("row", "col"), None),
        P(("row", "col"), None),
        P(("row", "col"), None),
        P(("row", "col"), None),
        P(),
    )
    out_specs = (P(("row", "col"), None), P(("row", "col"), None), P(("row", "col")))
    return jax.shard_map(local, mesh=mesh, in_specs=in_specs, out_specs=out_specs, check_vma=False)
```

time: 1370 us -> 707 us (0.52)
  matrix products: 487 us -> 142 us
  waiting for transfers between devices: 817 us -> 518 us
  other arithmetic: 23.6 us -> 9.56 us
    dot_general x2 -> x4, matrix products: 487 us -> 142 us  [the longest x2 136 us: local(): jnp.dot(ainv, colpanel, precision=lax.Precision.HIGH, preferred_element_t...]
    psum x1 -> x0, waiting for transfers between devices: 238 us -> none  [from_root(): return lax.psum(block, axis)]
    reduce_scatter x1 -> x2, waiting for transfers between devices: 113 us -> 52.5 us  [local(): lax.psum_scatter(term, 'col', scatter_dimension=0, tiled=False)]
    reduce_scatter x1 -> x2, waiting for transfers between devices: 244 us -> 189 us  [local(): lax.psum_scatter(partial_value, 'col', scatter_dimension=0, tiled=True)]
    all_gather x1 -> x2, waiting for transfers between devices: 223 us -> 258 us  [local(): lax.all_gather(to_grid_column(lmasked), 'row', axis=0, tiled=True)]
    unnamed x4 -> x8, waiting for transfers between devices: 0.07 us -> 18.7 us
  transfers between devices with their start and end apart: 4 -> 9, of which waited for: 4 -> 7; matrix products, arithmetic and copies ran while one was open for 2% -> 23% of each run, Pallas kernels for 0% -> 0%
where the time goes in v1:
time: 707 us; the launch traced here: 706 us
  waiting for transfers between devices  518 us (73%)
  matrix products  142 us (20%)
  local copies, waits for them, and re-layouts  20.1 us (3%)
  between operations  14.9 us (2%)
  other arithmetic  9.56 us (1%)
    all_gather x2, waiting for transfers between devices, local(): lax.all_gather(to_grid_column(lmasked), 'row', axis=0, tiled=True)  258 us
    reduce_scatter x2, waiting for transfers between devices, local(): lax.psum_scatter(partial_value, 'col', scatter_dimension=0, tiled=True)  189 us
    dot_general x2, matrix products, local(): jnp.dot(ainv, colpanel, precision=lax.Precision.HIGH, preferred_element_t...  136 us
    reduce_scatter x2, waiting for transfers between devices, local(): lax.psum_scatter(term, 'col', scatter_dimension=0, tiled=False)  52.5 us
    unnamed x8, waiting for transfers between devices  18.7 us
  transfers between devices with their start and end apart: 9, of which 7 were waited for; matrix products, arithmetic and copies ran while one was open for 23% of the time, Pallas kernels for 0%

profile of v1, /device:TPU:0, one launch (start us, length us, event | category | flops | bytes accessed | tf_op | source)
XLA Modules:
  0.0 706.4 jit_solution(5232533683457944852)
XLA Ops:
  7.2 0.8 convert_bitcast_fusion.3
  8.1 3.3 fusion
  11.4 0.5 copy.24
  12.0 0.8 collective-permute-start
  12.8 1.1 copy-done.3
  14.2 1.9 copy.25
  16.2 1.1 copy-done
  17.3 0.7 collective-permute-start.1
  18.1 1.1 copy-done.4
  19.3 253.5 %all-gather.3.cloned.1.call-done = f32[3072,512]{0,1:T(8,128)} async-done(((f32[768,512]{0,1:T(8,128)}), f32[3072,512]{0,1:T(8,128)}) %all-gather.3.cloned.1.call-update) | async-done | bytes 6291472 | tf_op jit(solution)/shard_map/all_gather | solution.py:32
  272.8 68.2 %convolution_bitcast_fusion.1 = f32[6144,512]{0,1:T(8,128)} fusion(f32[3072,512]{0,1:T(8,128)} %all-gather.3.cloned.1.call-done, f32[6144,3072]{1,0:T(8,128)} %param.7), kind=kOutput, calls=%fused_computation.1 | convolution fusion | flops 57982058496 | bytes 94371840 | tf_op jit(solution)/shard_map/dot_general | solution.py:33
  341.3 4.0 all-gather.5.cloned.1.call-done
  345.3 68.2 %convolution_bitcast_fusion = f32[6144,512]{0,1:T(8,128)} fusion(f32[3072,512]{0,1:T(8,128)} %all-gather.5.cloned.1.call-done, f32[6144,3072]{1,0:T(8,128)} %param.7), kind=kOutput, calls=%fused_computation | convolution fusion | flops 57982058496 | bytes 94371840 | tf_op jit(solution)/shard_map/dot_general | solution.py:33
  413.5 0.3 reduce-scatter.12.cloned.1.call-start
  413.8 63.0 %reduce-scatter.8.cloned.1.call-done = f32[768,512]{0,1:T(8,128)} async-done(((f32[6144,512]{0,1:T(8,128)}), f32[768,512]{0,1:T(8,128)}) %reduce-scatter.8.cloned.1.call-update) | async-done | bytes 1572880 | tf_op jit(solution)/shard_map/reduce_scatter | solution.py:36
  476.8 2.8 fusion.2
  479.6 1.1 copy.31
  480.7 125.8 %reduce-scatter.10.cloned.1.call-done = f32[768,512]{0,1:T(8,128)} async-done(((f32[6144,512]{0,1:T(8,128)}), f32[768,512]{0,1:T(8,128)}) %reduce-scatter.10.cloned.1.call-update) | async-done | bytes 1572880 | tf_op jit(solution)/shard_map/reduce_scatter | solution.py:36
  606.6 2.8 fusion.3
  609.4 1.1 copy.30
  610.5 3.3 fusion.1
  613.9 0.5 copy.26
  614.7 1.9 copy.27
  617.4 2.8 multiply_reduce_fusion.1
  620.2 19.6 %reduce-scatter.12.cloned.1.call-done = f32[1,2,32,512]{3,2,1,0:T(8,128)} async-done(((f32[8,2,32,512]{3,2,1,0:T(8,128)}), f32[1,2,32,512]{3,2,1,0:T(8,128)}) %reduce-scatter.12.cloned.1.call-update) | async-done | bytes 131088 | tf_op jit(solution)/shard_map/reduce_scatter | solution.py:43
  639.8 32.9 %reduce-scatter.14.cloned.1.call-done = f32[1,2,32,512]{3,2,1,0:T(8,128)} async-done(((f32[8,2,32,512]{3,2,1,0:T(8,128)}), f32[1,2,32,512]{3,2,1,0:T(8,128)}) %reduce-scatter.14.cloned.1.call-update) | async-done | bytes 131088 | tf_op jit(solution)/shard_map/reduce_scatter | solution.py:43
  672.7 1.7 pad_maximum_fusion.1
  674.4 1.8 multiply_reduce_fusion
  676.5 2.4 copy.23
  678.9 0.6 add_multiply_fusion
  679.5 18.6 %reduce-scatter.16.cloned.1.call-done = f32[1,32,512]{2,1,0:T(8,128)} async-done(((f32[4,32,512]{2,1,0:T(8,128)}), f32[1,32,512]{2,1,0:T(8,128)}) %reduce-scatter.16.cloned.1.call-update) | async-done | bytes 65552
  698.0 1.5 bitcast_add_fusion
  (38 shorter events, 1.8 us)
Async XLA Ops:
  7.2 265.7 %all-gather.3.cloned.1.call-start = ((), (), s32[]{:S(2)}) async-start(), calls=%async_computation.5 | async-start | bytes 7864320 | tf_op jit(solution)/shard_map/all_gather | solution.py:32
  12.0 0.8 collective-permute-start
  12.8 1.1 copy-start.3
  14.0 331.3 %all-gather.5.cloned.1.call-start = ((), (), s32[]{:S(2)}) async-start(), calls=%async_computation.7 | async-start | bytes 7864320 | tf_op jit(solution)/shard_map/all_gather | solution.py:32
  16.2 1.2 copy-start
  17.3 0.8 collective-permute-start.1
  18.1 1.1 copy-start.4
  19.3 457.5 %reduce-scatter.8.cloned.1.call-start = ((), (), s32[]{:S(2)}) async-start(), calls=%async_computation.6 | async-start | bytes 14155776 | tf_op jit(solution)/shard_map/reduce_scatter | solution.py:36
  341.1 265.5 %reduce-scatter.10.cloned.1.call-start = ((), (), s32[]{:S(2)}) async-start(), calls=%async_computation.8 | async-start | bytes 14155776 | tf_op jit(solution)/shard_map/reduce_scatter | solution.py:36
  413.5 226.2 %reduce-scatter.12.cloned.1.call-start = ((), (), s32[]{:S(2)}) async-start(), calls=%async_computation.9 | async-start | bytes 1179648 | tf_op jit(solution)/shard_map/reduce_scatter | solution.py:43
  479.6 127.0 %copy-start.1 = (f32[768,512]{0,1:T(8,128)S(1)}, f32[768,512]{0,1:T(8,128)}, u32[]{:S(2)}) copy-start(f32[768,512]{0,1:T(8,128)} %copy-done) | copy-start | bytes 4718596
  480.7 192.0 %reduce-scatter.14.cloned.1.call-start = ((), (), s32[]{:S(2)}) async-start(), calls=%async_computation.10 | async-start | bytes 1179648 | tf_op jit(solution)/shard_map/reduce_scatter | solution.py:43
  610.5 87.6 %reduce-scatter.16.cloned.1.call-start = ((), (), s32[]{:S(2)}) async-start(), calls=%async_computation.11 | async-start | bytes 327680
  613.9 0.7 copy-start.6
  674.4 1.9 copy-start.2
  676.5 21.5 %copy-start.5 = (f32[32,512]{1,0:T(8,128)S(1)}, f32[32,512]{1,0:T(8,128)}, u32[]{:S(2)}) copy-start(f32[32,512]{1,0:T(8,128)} %param.9) | copy-start | bytes 196612
Sparse Core Ops, SparseCore 0:
  14.1 258.6 all-gather.2
  275.2 70.0 all-gather.4
  347.6 129.1 reduce-scatter.7
  478.9 127.6 reduce-scatter.9
  608.7 31.0 reduce-scatter.11
  641.9 30.7 reduce-scatter.13
  675.5 22.5 reduce-scatter.15
